TPU v7x, 512 devices: a whole 4x4x16 slice. The times are simulated.
512 devices in a mesh: pairs: 128 (over x, z, core), rep: 4 (over y).
Axes of the slice: x: 4, y: 4, z: 16, core: 2. Of those that a mesh axis runs over, the one named last changes fastest.
Arguments:
- positions: float32 [3, 2048, 256], P(None, 'pairs'), may hold values from -1 to 1
- facing: float32 [2, 2048, 256], P(None, 'pairs'), may hold values from -3.140625 to 3.140625
- area: float32 [2048, 256], P('pairs'), may hold values from 0.00390625 to 0.03125
- emission: float32 [2048, 8, 256], P('pairs'), may hold values from 0.1 to 2
- reflect: float32 [2048, 8, 256], P('pairs'), may hold values from 0.2 to 0.9
- pair_list: int32 [128, 4, 128, 1, 2], P('pairs', 'rep'), may hold values from -1 to 2047, as said below
Outputs:
- radiosity: float32 [2048, 8, 256], P('pairs')
Inputs may be any that keep to these rules, and one draw needn't show every extreme that they name: `pair_list`: entry [p, r, q, c] is held by the device at pairs index p and rep index r in its slot c toward pairs index q. Its row block lies in p * 16 to (p + 1) * 16 - 1 and its column block in q * 16 to (q + 1) * 16 - 1, or both entries are -1 for an empty slot. Slots toward pairs index 0 are never empty.
All inputs are finite; a program needn't handle non-finite values.
Results may differ from a plain program's by a relative error of at most 0.0003.
Values may be sent and summed in bfloat16 or wider, within the bound.
A program may use at most 64 MiB of HBM per device.

v0:
```python
import jax
import jax.numpy as jnp
from jax import lax
from jax.sharding import PartitionSpec as P

SWEEPS = 2
soften = 0.1
group_tiles = 8


def unit_normals(facing):
    azimuth = facing[0]
    elevation = facing[1]
    return jnp.stack(
        [
            jnp.cos(azimuth) * jnp.cos(elevation),
            jnp.sin(azimuth) * jnp.cos(elevation),
            jnp.sin(elevation),
        ],
        axis=0,
    )


def pack_geometry(positions, facing):
    normals = unit_normals(facing)
    return jnp.transpose(jnp.concatenate([positions, normals], axis=0), (1, 0, 2))


def coupling(row_geom, col_geom):
    offsets = [
        col_geom[:, axis_id, None, :] - row_geom[:, axis_id, :, None] for axis_id in range(3)
    ]
    spread = offsets[0] * offsets[0] + offsets[1] * offsets[1] + offsets[2] * offsets[2] + soften
    nearside = (
        row_geom[:, 3, :, None] * offsets[0]
        + row_geom[:, 4, :, None] * offsets[1]
        + row_geom[:, 5, :, None] * offsets[2]
    )
    farside = (
        col_geom[:, 3, None, :] * offsets[0]
        + col_geom[:, 4, None, :] * offsets[1]
        + col_geom[:, 5, None, :] * offsets[2]
    )
    coupled = jnp.maximum(nearside, 0.0) * jnp.maximum(-farside, 0.0) / (jnp.pi * spread * spread)
    return coupled.astype(jnp.bfloat16)


def compact(active):
    slots = active.shape[0]
    flags = active.astype(jnp.int32)
    live_count = jnp.sum(flags)
    position = jnp.where(active, jnp.cumsum(flags) - 1, slots + group_tiles)
    ordering = jnp.full((slots + group_tiles,), slots, jnp.int32)
    ordering = ordering.at[position].set(jnp.arange(slots, dtype=jnp.int32), mode="drop")
    return (ordering, live_count)


def over_tiles(ordering, live_count, visit, initial):
    turns = (live_count + group_tiles - 1) // group_tiles

    def one_turn(turn_index, carry):
        slot_ids = lax.dynamic_slice_in_dim(ordering, turn_index * group_tiles, group_tiles)
        return visit(carry, slot_ids)

    return lax.fori_loop(0, turns, one_turn, initial)


def block_sum(block_ids, valid, terms, blocks):
    selector = (
        (block_ids[:, None] == jnp.arange(blocks, dtype=jnp.int32)[None, :]) & valid[:, None]
    ).astype(jnp.float32)
    return jnp.einsum("gk,gbi->kbi", selector, terms, precision=lax.Precision.HIGHEST)


def pair_kernel(slot_ids, row_local, geometry, col_geometry):
    slots = row_local.shape[0]
    valid = slot_ids < slots
    safe = jnp.minimum(slot_ids, slots - 1)
    row_ids = jnp.where(valid, jnp.take(row_local, safe), 0)
    kernel = coupling(jnp.take(geometry, row_ids, axis=0), jnp.take(col_geometry, safe, axis=0))
    return (valid, safe, row_ids, kernel)


def shards(positions, facing, area, emission, reflect, pair_list):
    blocks = area.shape[0]
    bands = emission.shape[1]
    patches = emission.shape[2]
    owners = lax.axis_size("pairs")
    geometry = pack_geometry(positions, facing)
    held = pair_list[0, 0]
    capacity = held.shape[1]
    slots = owners * capacity
    row_local = jnp.where(held[:, :, 0] >= 0, held[:, :, 0] % blocks, -1).reshape(slots)
    col_local = jnp.where(held[:, :, 1] >= 0, held[:, :, 1] % blocks, -1)
    requests = lax.all_to_all(col_local, "pairs", split_axis=0, concat_axis=0, tiled=True)
    served = jnp.take(geometry, jnp.clip(requests, 0, blocks - 1), axis=0)
    col_geometry = lax.all_to_all(served, "pairs", split_axis=0, concat_axis=0, tiled=True).reshape(
        slots, 6, patches
    )
    ordering, live_count = compact(row_local >= 0)
    wanted = requests.reshape(slots)
    owner_select = (wanted[:, None] == jnp.arange(blocks, dtype=jnp.int32)[None, :]).astype(
        jnp.float32
    )
    empty_sum = jnp.zeros((blocks, bands, patches), jnp.float32)
    radiosity = emission
    for sweep_index in range(SWEEPS):
        weighted = (area[:, None, :] * radiosity).astype(jnp.bfloat16)
        served_weights = jnp.take(weighted, jnp.clip(requests, 0, blocks - 1), axis=0)
        fetched = lax.all_to_all(served_weights, "pairs", split_axis=0, concat_axis=0, tiled=True)
        col_weights = fetched.reshape(slots, bands, patches)

        def both_visit(carry, slot_ids):
            row_part, returned = carry
            valid, safe, row_ids, kernel = pair_kernel(slot_ids, row_local, geometry, col_geometry)
            row_terms = jnp.einsum(
                "gij,gbj->gbi",
                kernel,
                jnp.take(col_weights, safe, axis=0),
                preferred_element_type=jnp.float32,
            )
            col_terms = jnp.einsum(
                "gij,gbi->gbj",
                kernel,
                jnp.take(weighted, row_ids, axis=0),
                preferred_element_type=jnp.float32,
            )
            row_part = row_part + block_sum(row_ids, valid, row_terms, blocks)
            returned = returned.at[jnp.where(valid, slot_ids, slots)].set(col_terms, mode="drop")
            return (row_part, returned)

        row_sum, returned = over_tiles(
            ordering,
            live_count,
            both_visit,
            (empty_sum, jnp.zeros((slots, bands, patches), jnp.float32)),
        )
        landed = lax.all_to_all(
            returned.reshape(owners, capacity, bands, patches),
            "pairs",
            split_axis=0,
            concat_axis=0,
            tiled=True,
        )
        incoming = jnp.einsum(
            "sk,sbp->kbp",
            owner_select,
            landed.reshape(slots, bands, patches),
            precision=lax.Precision.HIGHEST,
        )
        gathered = lax.psum(row_sum + incoming, "rep")
        radiosity = emission + reflect * gathered
    return radiosity


def solution(mesh):
    placed = (
        P(None, "pairs", None),
        P(None, "pairs", None),
        P("pairs", None),
        P("pairs", None, None),
        P("pairs", None, None),
        P("pairs", "rep", None, None, None),
    )
    return jax.shard_map(
        shards, mesh=mesh, in_specs=placed, out_specs=P("pairs", None, None), check_vma=False
    )
```

profile of v0, /device:TPU:2, one launch (start us, length us, event | category | flops | bytes accessed | tf_op | source)
XLA Modules:
  0.0 799.7 jit_solution(11148665395816167960)
XLA Ops:
  10.4 19.5 %all-to-all-start = ((s32[128,1,1]{2,1,0:T(1,128)}), s32[128,1,1]{2,1,0:T(1,128)S(1)}, u32[]{:S(2)}, u32[]{:S(2)}) async-start(s32[128,1,1]{2,1,0:T(1,128)} %get-tuple-element.351), calls=%async_computation | async-start | bytes 131072 | tf_op jit(solution)/shard_map/all_to_all | solution.py:95
  31.8 12.5 %all-to-all-done = s32[128,1,1]{2,1,0:T(1,128)S(1)} async-done(((s32[128,1,1]{2,1,0:T(1,128)}), s32[128,1,1]{2,1,0:T(1,128)S(1)}, u32[]{:S(2)}, u32[]{:S(2)}) %all-to-all-start) | async-done | bytes 544 | tf_op jit(solution)/shard_map/all_to_all | solution.py:95
  51.9 7.4 all-to-all-start.2
  59.4 4.6 fusion.83
  65.7 38.4 %all-to-all-done.2 = f32[128,1,6,256]{3,1,2,0:T(1,128)S(1)} async-done(((f32[128,1,6,256]{3,1,2,0:T(1,128)}), f32[128,1,6,256]{3,1,2,0:T(1,128)S(1)}, u32[]{:S(2)}, u32[]{:S(2)}) %all-to-all-start.2) | async-done | bytes 786464 | tf_op jit(solution)/shard_map/all_to_all | solution.py:97
  104.1 6.7 all-to-all-start.1
  113.7 30.7 %all-to-all-done.1 = bf16[128,1,8,256]{3,2,1,0:T(8,128)(2,1)S(1)} async-done(((bf16[128,1,8,256]{3,2,1,0:T(8,128)(2,1)}), bf16[128,1,8,256]{3,2,1,0:T(8,128)(2,1)S(1)}, u32[]{:S(2)}, u32[]{:S(2)}) %all-to-all-start.1) | async-done | bytes 524320 | tf_op jit(solution)/shard_map/all_to_all | solution.py:110
  144.5 57.7 %while.24 = (s32[]{:T(128)}, f32[16,8,256]{2,0,1:T(8,128)S(1)}, f32[128,8,256]{2,1,0:T(8,128)S(1)}, s32[]{:T(128)}, s32[136]{0:T(256)S(1)}, /*index=5*/s32[128]{...) while((s32[]{:T(128)}, f32[16,8,256]{2,0,1:T(8,128)S(1)}, ...), condition=%wide.region_5.12_spmd, body=%wide.region_3.11_spmd.sunk | while | flops 48327124 | bytes 1844099 | solution.py:65
  147.4 3.5 fusion.119
  152.2 3.5 fusion.118
  158.9 3.5 fusion.119
  163.7 3.5 fusion.118
  170.4 3.5 fusion.119
  175.3 3.5 fusion.118
  182.0 3.5 fusion.119
  186.8 3.5 fusion.118
  193.5 3.5 fusion.119
  198.3 3.5 fusion.118
  202.2 189.1 %all_to_all.31 = f32[128,1,8,256]{3,2,1,0:T(8,128)S(1)} all-to-all(f32[128,1,8,256]{3,2,1,0:T(8,128)S(1)} %bitcast.135), channel_id=1, replica_groups=mesh['pairs'=128,'rep'=4] {'pairs'}, dimensions={0} | all-to-all | bytes 2097152 | tf_op jit(solution)/shard_map/all_to_all | solution.py:138
  392.7 49.1 %all-reduce.3.cloned.1.call-done = f32[16,8,256]{2,0,1:T(8,128)} async-done(((f32[16,8,256]{2,0,1:T(8,128)}), f32[16,8,256]{2,0,1:T(8,128)}) %all-reduce.3.cloned.1.call-update) | async-done | bytes 131088 | tf_op jit(solution)/shard_map/psum | solution.py:151
  444.5 16.6 %all-to-all-start.4 = ((bf16[128,1,8,256]{3,2,1,0:T(8,128)(2,1)}), bf16[128,1,8,256]{3,2,1,0:T(8,128)(2,1)S(1)}, u32[]{:S(2)}, u32[]{:S(2)}) async-start(bf16[128,1,8,256]{3,2,1,0:T(8,128)(2,1)} %fusion.66), calls=%async_computation.4 | async-start | bytes 1048576 | tf_op jit(solution)/shard_map/all_to_all | solution.py:110
  461.2 33.5 %all-to-all-done.4 = bf16[128,1,8,256]{3,2,1,0:T(8,128)(2,1)S(1)} async-done(((bf16[128,1,8,256]{3,2,1,0:T(8,128)(2,1)}), bf16[128,1,8,256]{3,2,1,0:T(8,128)(2,1)S(1)}, u32[]{:S(2)}, u32[]{:S(2)}) %all-to-all-start.4) | async-done | bytes 524320 | tf_op jit(solution)/shard_map/all_to_all | solution.py:110
  494.8 57.7 %while.25 = (s32[]{:T(128)}, f32[16,8,256]{2,0,1:T(8,128)S(1)}, f32[128,8,256]{2,1,0:T(8,128)S(1)}, s32[]{:T(128)}, s32[136]{0:T(256)S(1)}, /*index=5*/s32[128]{...) while((s32[]{:T(128)}, f32[16,8,256]{2,0,1:T(8,128)S(1)}, ...), condition=%wide.region_9.16_spmd, body=%wide.region_7.15_spmd.sunk | while | flops 48327124 | bytes 1844099 | solution.py:65
  497.7 3.5 fusion.129
  509.2 3.5 fusion.129
  514.0 3.5 fusion.128
  520.8 3.5 fusion.129
  525.6 3.5 fusion.128
  532.3 3.5 fusion.129
  543.8 3.5 fusion.129
  552.5 189.1 %all_to_all.32 = f32[128,1,8,256]{3,2,1,0:T(8,128)S(1)} all-to-all(f32[128,1,8,256]{3,2,1,0:T(8,128)S(1)} %bitcast.134), channel_id=1, replica_groups=mesh['pairs'=128,'rep'=4] {'pairs'}, dimensions={0} | all-to-all | bytes 2097152 | tf_op jit(solution)/shard_map/all_to_all | solution.py:138
  743.0 48.1 %all-reduce.5.cloned.1.call-done = f32[16,8,256]{2,0,1:T(8,128)} async-done(((f32[16,8,256]{2,0,1:T(8,128)}), f32[16,8,256]{2,0,1:T(8,128)}) %all-reduce.5.cloned.1.call-update) | async-done | bytes 131088 | tf_op jit(solution)/shard_map/psum | solution.py:151
  (283 shorter events, 78.5 us)
Async XLA Ops:
  10.4 33.9 %all-to-all-start = ((s32[128,1,1]{2,1,0:T(1,128)}), s32[128,1,1]{2,1,0:T(1,128)S(1)}, u32[]{:S(2)}, u32[]{:S(2)}) async-start(s32[128,1,1]{2,1,0:T(1,128)} %get-tuple-element.351), calls=%async_computation | async-start | bytes 131072 | tf_op jit(solution)/shard_map/all_to_all | solution.py:95
  51.8 7.4 copy-start
  51.9 7.4 copy-start.2
  51.9 52.3 %all-to-all-start.2 = ((f32[128,1,6,256]{3,1,2,0:T(1,128)}), f32[128,1,6,256]{3,1,2,0:T(1,128)S(1)}, u32[]{:S(2)}, u32[]{:S(2)}) async-start(f32[128,1,6,256]{3,1,2,0:T(1,128)} %copy.141), calls=%async_computation.2 | async-start | bytes 1572864 | tf_op jit(solution)/shard_map/all_to_all | solution.py:97
  104.1 40.3 %all-to-all-start.1 = ((bf16[128,1,8,256]{3,2,1,0:T(8,128)(2,1)}), bf16[128,1,8,256]{3,2,1,0:T(8,128)(2,1)S(1)}, u32[]{:S(2)}, u32[]{:S(2)}) async-start(bf16[128,1,8,256]{3,2,1,0:T(8,128)(2,1)} %fusion.67), calls=%async_computation.1 | async-start | bytes 1048576 | tf_op jit(solution)/shard_map/all_to_all | solution.py:110
  110.8 331.1 %all-reduce.3.cloned.1.call-start = ((), (), s32[]{:S(2)}) async-start(), calls=%async_computation.6 | async-start | bytes 262144 | tf_op jit(solution)/shard_map/psum | solution.py:151
  391.3 50.6 %copy-start.1 = (f32[16,8,256]{2,1,0:T(8,128)S(1)}, f32[16,8,256]{2,1,0:T(8,128)}, u32[]{:S(2)}) copy-start(f32[16,8,256]{2,1,0:T(8,128)} %param.26) | copy-start | bytes 393220
  444.5 50.2 %all-to-all-start.4 = ((bf16[128,1,8,256]{3,2,1,0:T(8,128)(2,1)}), bf16[128,1,8,256]{3,2,1,0:T(8,128)(2,1)S(1)}, u32[]{:S(2)}, u32[]{:S(2)}) async-start(bf16[128,1,8,256]{3,2,1,0:T(8,128)(2,1)} %fusion.66), calls=%async_computation.4 | async-start | bytes 1048576 | tf_op jit(solution)/shard_map/all_to_all | solution.py:110
  461.2 329.9 %all-reduce.5.cloned.1.call-start = ((), (), s32[]{:S(2)}) async-start(), calls=%async_computation.7 | async-start | bytes 262144 | tf_op jit(solution)/shard_map/psum | solution.py:151
Sparse Core Ops, SparseCore 0:
  392.8 48.9 all-reduce.2
  743.1 47.9 all-reduce.4
where the time goes:
time: 800 us
  blocking collectives  378 us (47%)
  waiting for transfers between devices  212 us (26%)
  matrix products  76.4 us (10%)
  starting transfers between devices  50.3 us (6%)
  local copies, waits for them, and re-layouts  44.2 us (6%)
  other arithmetic  22.1 us (3%)
  between operations  14.3 us (2%)
    all_to_all x2, blocking collectives, shards(): lax.all_to_all(returned.reshape(owners, capacity, bands, patches), 'pairs...  378 us
    psum x2, waiting for transfers between devices, shards(): gathered = lax.psum(row_sum + incoming, 'rep')  97.3 us
    all_to_all x2, waiting for transfers between devices, shards(): lax.all_to_all(served_weights, 'pairs', split_axis=0, concat_axis=0, tile...  64.3 us
    all_to_all x1, waiting for transfers between devices, shards(): lax.all_to_all(served, 'pairs', split_axis=0, concat_axis=0, tiled=True)  38.4 us
    dot_general x10, matrix products, both_visit(): jnp.einsum('gij,gbi->gbj', kernel, jnp.take(weighted, row_ids, axis=0), p...  35.2 us
    dot_general x10, matrix products, both_visit(): jnp.einsum('gij,gbj->gbi', kernel, jnp.take(col_weights, safe, axis=0), p...  35 us
    all_to_all x2, starting transfers between devices, shards(): lax.all_to_all(served_weights, 'pairs', split_axis=0, concat_axis=0, tile...  23.3 us
    all_to_all x1, starting transfers between devices, shards(): lax.all_to_all(col_local, 'pairs', split_axis=0, concat_axis=0, tiled=True)  19.5 us
  transfers between devices with their start and end apart: 6, of which 6 were waited for; matrix products, arithmetic and copies ran while one was open for 1% of the time, Pallas kernels for 0%

commit v1 on v0

--- a/solution.py
+++ b/solution.py
@@ -148,7 +148,7 @@
             landed.reshape(slots, bands, patches),
             precision=lax.Precision.HIGHEST,
         )
-        gathered = lax.psum(row_sum + incoming, "rep")
+        gathered = lax.all_gather(row_sum + incoming, "rep").sum(axis=0)
         radiosity = emission + reflect * gathered
     return radiosity
 

time: 800 us -> 703 us (0.88)
  waiting for transfers between devices: 212 us -> 115 us
  blocking collectives: 378 us -> 405 us
  between operations: 14.3 us -> 0.94 us
  starting transfers between devices: 50.3 us -> 40.4 us
    psum x2 -> x0, waiting for transfers between devices: 97.3 us -> none  [shards(): gathered = lax.psum(row_sum + incoming, 'rep')]
    all_gather x0 -> x2, blocking collectives: none -> 27.3 us  [shards(): gathered = lax.all_gather(row_sum + incoming, 'rep').sum(axis=0)]
    all_to_all x2, starting transfers between devices: 23.3 us -> 13.5 us  [shards(): lax.all_to_all(served_weights, 'pairs', split_axis=0, concat_axis=0, tile...]
  transfers between devices with their start and end apart: 6 -> 4, of which waited for: 6 -> 4; matrix products, arithmetic and copies ran while one was open for 1% -> 1% of each run, Pallas kernels for 0% -> 0%
where the time goes in v1:
time: 703 us
  blocking collectives  405 us (58%)
  waiting for transfers between devices  115 us (16%)
  matrix products  74.8 us (11%)
  local copies, waits for them, and re-layouts  44.2 us (6%)
  starting transfers between devices  40.4 us (6%)
  other arithmetic  20.3 us (3%)
    all_to_all x2, blocking collectives, shards(): lax.all_to_all(returned.reshape(owners, capacity, bands, patches), 'pairs...  378 us
    all_to_all x2, waiting for transfers between devices, shards(): lax.all_to_all(served_weights, 'pairs', split_axis=0, concat_axis=0, tile...  64.4 us
    all_to_all x1, waiting for transfers between devices, shards(): lax.all_to_all(served, 'pairs', split_axis=0, concat_axis=0, tiled=True)  38.5 us
    dot_general x10, matrix products, both_visit(): jnp.einsum('gij,gbi->gbj', kernel, jnp.take(weighted, row_ids, axis=0), p...  35 us
    dot_general x10, matrix products, both_visit(): jnp.einsum('gij,gbj->gbi', kernel, jnp.take(col_weights, safe, axis=0), p...  34.9 us
    all_gather x2, blocking collectives, shards(): gathered = lax.all_gather(row_sum + incoming, 'rep').sum(axis=0)  27.3 us
    all_to_all x1, starting transfers between devices, shards(): lax.all_to_all(col_local, 'pairs', split_axis=0, concat_axis=0, tiled=True)  19.5 us
  transfers between devices with their start and end apart: 4, of which 4 were waited for; matrix products, arithmetic and copies ran while one was open for 1% of the time, Pallas kernels for 0%

profile of v1, /device:TPU:2, one launch (start us, length us, event | category | flops | bytes accessed | tf_op | source)
XLA Modules:
  0.0 702.5 jit_solution(17231585219399181316)
XLA Ops:
  3.9 19.5 %all-to-all-start = ((s32[128,1,1]{2,1,0:T(1,128)}), s32[128,1,1]{2,1,0:T(1,128)S(1)}, u32[]{:S(2)}, u32[]{:S(2)}) async-start(s32[128,1,1]{2,1,0:T(1,128)} %get-tuple-element.311), calls=%async_computation | async-start | bytes 131072 | tf_op jit(solution)/shard_map/all_to_all | solution.py:95
  25.3 12.5 %all-to-all-done = s32[128,1,1]{2,1,0:T(1,128)S(1)} async-done(((s32[128,1,1]{2,1,0:T(1,128)}), s32[128,1,1]{2,1,0:T(1,128)S(1)}, u32[]{:S(2)}, u32[]{:S(2)}) %all-to-all-start) | async-done | bytes 544 | tf_op jit(solution)/shard_map/all_to_all | solution.py:95
  45.3 7.4 %all-to-all-start.2 = ((f32[128,1,6,256]{3,1,2,0:T(1,128)}), f32[128,1,6,256]{3,1,2,0:T(1,128)S(1)}, u32[]{:S(2)}, u32[]{:S(2)}) async-start(f32[128,1,6,256]{3,1,2,0:T(1,128)} %copy.105), calls=%async_computation.2 | async-start | bytes 1572864 | tf_op jit(solution)/shard_map/all_to_all | solution.py:97
  52.8 4.6 fusion.86
  59.1 38.5 %all-to-all-done.2 = f32[128,1,6,256]{3,1,2,0:T(1,128)S(1)} async-done(((f32[128,1,6,256]{3,1,2,0:T(1,128)}), f32[128,1,6,256]{3,1,2,0:T(1,128)S(1)}, u32[]{:S(2)}, u32[]{:S(2)}) %all-to-all-start.2) | async-done | bytes 786464 | tf_op jit(solution)/shard_map/all_to_all | solution.py:97
  97.6 6.7 all-to-all-start.1
  107.1 30.8 %all-to-all-done.1 = bf16[128,1,8,256]{3,2,1,0:T(8,128)(2,1)S(1)} async-done(((bf16[128,1,8,256]{3,2,1,0:T(8,128)(2,1)}), bf16[128,1,8,256]{3,2,1,0:T(8,128)(2,1)S(1)}, u32[]{:S(2)}, u32[]{:S(2)}) %all-to-all-start.1) | async-done | bytes 524320 | tf_op jit(solution)/shard_map/all_to_all | solution.py:110
  138.0 57.5 %while.24 = (s32[]{:T(128)}, f32[16,8,256]{2,0,1:T(8,128)S(1)}, f32[128,8,256]{2,1,0:T(8,128)S(1)}, s32[]{:T(128)}, s32[136]{0:T(256)S(1)}, /*index=5*/s32[128]{...) while((s32[]{:T(128)}, f32[16,8,256]{2,0,1:T(8,128)S(1)}, ...), condition=%wide.region_5.12_spmd, body=%wide.region_3.11_spmd.sunk | while | flops 48327124 | bytes 1844099 | solution.py:65
  140.8 3.5 fusion.122
  145.6 3.5 fusion.121
  152.3 3.5 fusion.122
  157.1 3.5 fusion.121
  163.8 3.5 fusion.122
  175.4 3.5 fusion.122
  186.9 3.5 fusion.122
  195.5 188.7 %all_to_all.31 = f32[128,1,8,256]{3,2,1,0:T(8,128)S(1)} all-to-all(f32[128,1,8,256]{3,2,1,0:T(8,128)S(1)} %bitcast.136), channel_id=1, replica_groups=mesh['pairs'=128,'rep'=4] {'pairs'}, dimensions={0} | all-to-all | bytes 2097152 | tf_op jit(solution)/shard_map/all_to_all | solution.py:138
  385.0 14.0 %all-gather = f32[64,8,256]{2,0,1:T(8,128)S(1)} all-gather(f32[16,8,256]{2,0,1:T(8,128)S(1)} %convolution_add_fusion.3), channel_id=2, replica_groups=mesh['pairs'=128,'rep'=4] {'rep'}, dimensions={0}, use_global_device_ids=true | all-gather | bytes 655360 | tf_op jit(solution)/shard_map/all_gather | solution.py:151
  400.8 6.8 all-to-all-start.4
  407.6 33.6 %all-to-all-done.4 = bf16[128,1,8,256]{3,2,1,0:T(8,128)(2,1)S(1)} async-done(((bf16[128,1,8,256]{3,2,1,0:T(8,128)(2,1)}), bf16[128,1,8,256]{3,2,1,0:T(8,128)(2,1)S(1)}, u32[]{:S(2)}, u32[]{:S(2)}) %all-to-all-start.4) | async-done | bytes 524320 | tf_op jit(solution)/shard_map/all_to_all | solution.py:110
  441.3 57.6 %while.25 = (s32[]{:T(128)}, f32[16,8,256]{2,0,1:T(8,128)S(1)}, f32[128,8,256]{2,1,0:T(8,128)S(1)}, s32[]{:T(128)}, s32[136]{0:T(256)S(1)}, /*index=5*/s32[128]{...) while((s32[]{:T(128)}, f32[16,8,256]{2,0,1:T(8,128)S(1)}, ...), condition=%wide.region_9.16_spmd, body=%wide.region_7.15_spmd.sunk | while | flops 48327124 | bytes 1844099 | solution.py:65
  444.1 3.5 fusion.132
  448.9 3.5 fusion.131
  455.7 3.5 fusion.132
  460.4 3.5 fusion.131
  467.2 3.5 fusion.132
  472.0 3.5 fusion.131
  478.7 3.5 fusion.132
  483.5 3.5 fusion.131
  490.2 3.5 fusion.132
  495.0 3.5 fusion.131
  498.8 188.8 %all_to_all.32 = f32[128,1,8,256]{3,2,1,0:T(8,128)S(1)} all-to-all(f32[128,1,8,256]{3,2,1,0:T(8,128)S(1)} %bitcast.137), channel_id=1, replica_groups=mesh['pairs'=128,'rep'=4] {'pairs'}, dimensions={0} | all-to-all | bytes 2097152 | tf_op jit(solution)/shard_map/all_to_all | solution.py:138
  688.3 13.3 %all-gather.1 = f32[64,8,256]{2,0,1:T(8,128)S(1)} all-gather(f32[16,8,256]{2,0,1:T(8,128)S(1)} %convolution_add_fusion.2), channel_id=3, replica_groups=mesh['pairs'=128,'rep'=4] {'rep'}, dimensions={0}, use_global_device_ids=true | all-gather | bytes 655360 | tf_op jit(solution)/shard_map/all_gather | solution.py:151
  (279 shorter events, 75.2 us)
Async XLA Ops:
  3.9 33.9 %all-to-all-start = ((s32[128,1,1]{2,1,0:T(1,128)}), s32[128,1,1]{2,1,0:T(1,128)S(1)}, u32[]{:S(2)}, u32[]{:S(2)}) async-start(s32[128,1,1]{2,1,0:T(1,128)} %get-tuple-element.311), calls=%async_computation | async-start | bytes 131072 | tf_op jit(solution)/shard_map/all_to_all | solution.py:95
  45.3 7.4 %copy-start = (f32[16,8,256]{2,1,0:T(8,128)S(1)}, f32[16,8,256]{2,1,0:T(8,128)}, u32[]{:S(2)}) copy-start(f32[16,8,256]{2,1,0:T(8,128)} %param.25) | copy-start | bytes 393220
  45.3 7.4 %copy-start.2 = (f32[16,256]{1,0:T(8,128)S(1)}, f32[16,256]{1,0:T(8,128)}, u32[]{:S(2)}) copy-start(f32[16,256]{1,0:T(8,128)} %param.24) | copy-start | bytes 49156
  45.3 52.3 %all-to-all-start.2 = ((f32[128,1,6,256]{3,1,2,0:T(1,128)}), f32[128,1,6,256]{3,1,2,0:T(1,128)S(1)}, u32[]{:S(2)}, u32[]{:S(2)}) async-start(f32[128,1,6,256]{3,1,2,0:T(1,128)} %copy.105), calls=%async_computation.2 | async-start | bytes 1572864 | tf_op jit(solution)/shard_map/all_to_all | solution.py:97
  97.6 40.3 %all-to-all-start.1 = ((bf16[128,1,8,256]{3,2,1,0:T(8,128)(2,1)}), bf16[128,1,8,256]{3,2,1,0:T(8,128)(2,1)S(1)}, u32[]{:S(2)}, u32[]{:S(2)}) async-start(bf16[128,1,8,256]{3,2,1,0:T(8,128)(2,1)} %fusion.67), calls=%async_computation.1 | async-start | bytes 1048576 | tf_op jit(solution)/shard_map/all_to_all | solution.py:110
  384.2 14.8 %copy-start.1 = (f32[16,8,256]{2,1,0:T(8,128)S(1)}, f32[16,8,256]{2,1,0:T(8,128)}, u32[]{:S(2)}) copy-start(f32[16,8,256]{2,1,0:T(8,128)} %param.26) | copy-start | bytes 393220
  400.8 40.4 %all-to-all-start.4 = ((bf16[128,1,8,256]{3,2,1,0:T(8,128)(2,1)}), bf16[128,1,8,256]{3,2,1,0:T(8,128)(2,1)S(1)}, u32[]{:S(2)}, u32[]{:S(2)}) async-start(bf16[128,1,8,256]{3,2,1,0:T(8,128)(2,1)} %fusion.66), calls=%async_computation.4 | async-start | bytes 1048576 | tf_op jit(solution)/shard_map/all_to_all | solution.py:110
